TPU v7x, 256 devices: a whole 4x4x8 slice. The times are simulated.
256 devices in a mesh: expert: 32 (over z, y), edata: 8 (over x, core).
Axes of the slice: x: 4, y: 4, z: 8, core: 2. Of those that a mesh axis runs over, the one named last changes fastest.
Arguments:
- tokens: bfloat16 [8192, 2048], P(('expert', 'edata')), may hold values from -6 to 6
- out_grad: bfloat16 [8192, 2048], P(('expert', 'edata')), may hold values from -6 to 6
- routes: int32 [8192, 8], P(('expert', 'edata')), may hold values from 0 to 31, as said below
- gate_codes: int32 [8192, 8], P(('expert', 'edata')), may hold values from 1 to 4095
- w_gate: bfloat16 [32, 2048, 768], P('expert'), may hold values from -0.125 to 0.125
- w_up: bfloat16 [32, 2048, 768], P('expert'), may hold values from -0.125 to 0.125
- w_down: bfloat16 [32, 768, 2048], P('expert'), may hold values from -0.21875 to 0.21875
Outputs:
- mixed: bfloat16 [8192, 2048], P(('expert', 'edata'))
- input_grad: bfloat16 [8192, 2048], P(('expert', 'edata'))
- grad_down: float32 [2048, 32, 768], P('edata', 'expert')
Inputs may be any that keep to these rules, and one draw needn't show every extreme that they name: `routes`: each token names 8 different experts. For each index of edata one expert, drawn anew in each draw, is named by exactly 16 of the 32 tokens of every device of that index of edata; any other expert is named by at most (8) tokens of one device.
All inputs are finite; a program needn't handle non-finite values.
Results may differ from a plain program's by a relative error of at most 0.017.
Values may be sent and summed in bfloat16 or wider, within the bound.
A program may use at most 128 MiB of HBM per device.

v0:
```python
import jax
import jax.numpy as jnp
from jax import lax
from jax.sharding import PartitionSpec as P

BLOCK = 128


def take_rows(source, row_ids, row_limit):
    is_valid = row_ids < row_limit
    safe_rows = jnp.minimum(row_ids, row_limit - 1)
    return jnp.where(
        is_valid[:, None], jnp.take(source, safe_rows, axis=0), jnp.zeros((), source.dtype)
    )


def expert_block(rows_in, grads_in, gate_mat, up_mat, down_mat):
    gate_pre = jnp.dot(rows_in, gate_mat, preferred_element_type=jnp.float32)
    up_pre = jnp.dot(rows_in, up_mat, preferred_element_type=jnp.float32)
    sig_gate = jax.nn.sigmoid(gate_pre)
    act_gate = gate_pre * sig_gate
    hidden_act = (act_gate * up_pre).astype(jnp.bfloat16)
    expert_out = jnp.dot(hidden_act, down_mat, preferred_element_type=jnp.float32).astype(
        jnp.bfloat16
    )
    grad_hidden = jnp.einsum("rd,fd->rf", grads_in, down_mat, preferred_element_type=jnp.float32)
    grad_gate_pre = (grad_hidden * up_pre * sig_gate * (1.0 + gate_pre * (1.0 - sig_gate))).astype(
        jnp.bfloat16
    )
    grad_up_pre = (grad_hidden * act_gate).astype(jnp.bfloat16)
    grad_rows = (
        jnp.einsum("rf,df->rd", grad_gate_pre, gate_mat, preferred_element_type=jnp.float32)
        + jnp.einsum("rf,df->rd", grad_up_pre, up_mat, preferred_element_type=jnp.float32)
    ).astype(jnp.bfloat16)
    return (expert_out, grad_rows, hidden_act)


def expert_sums(rows_do, rows_hidden, rows_owner):
    keep_mask = (rows_owner == 0).astype(jnp.bfloat16)
    terms = [
        jnp.einsum(
            "rd,rf->df", rows_do, rows_hidden * keep_mask, preferred_element_type=jnp.float32
        )
    ]
    return jnp.stack(terms, axis=1)


def shards(tokens, out_grad, routes, gate_codes, w_gate, w_up, w_down):
    tok_rows, model_width = tokens.shape
    top_count = routes.shape[1]
    local_experts = w_gate.shape[0]
    hidden_units = w_gate.shape[2]
    n_expert = lax.axis_size("expert")
    all_experts = local_experts * n_expert
    capacity = 2 * tok_rows * top_count // all_experts
    routed = tok_rows * top_count
    buffer_rows = all_experts * capacity
    gate_float = gate_codes.astype(jnp.float32)
    gate_values = gate_float / jnp.sum(gate_float, axis=1, keepdims=True)
    scaled = (
        (gate_values[:, :, None] * out_grad[:, None, :].astype(jnp.float32))
        .astype(jnp.bfloat16)
        .reshape(routed, model_width)
    )
    flat_expert = routes.reshape(routed)
    onehot = (flat_expert[:, None] == jnp.arange(all_experts, dtype=jnp.int32)[None, :]).astype(
        jnp.int32
    )
    before = jnp.cumsum(onehot, axis=0) - onehot
    slot_of = jnp.sum(before * onehot, axis=1)
    counts = jnp.sum(onehot, axis=0)
    target = flat_expert * capacity + slot_of
    owner_row = (
        jnp.full((buffer_rows,), routed, jnp.int32)
        .at[target]
        .set(jnp.arange(routed, dtype=jnp.int32))
    )
    token_of = jnp.where(owner_row < routed, owner_row // top_count, tok_rows)
    send_x = take_rows(tokens, token_of, tok_rows).reshape(all_experts, capacity, model_width)
    send_do = take_rows(scaled, owner_row, routed).reshape(all_experts, capacity, model_width)
    send_count = counts.astype(jnp.bfloat16).reshape(all_experts, 1)
    recv_x, recv_do, recv_count = (
        lax.all_to_all(send_x, "expert", split_axis=0, concat_axis=0, tiled=True),
        lax.all_to_all(send_do, "expert", split_axis=0, concat_axis=0, tiled=True),
        lax.all_to_all(send_count, "expert", split_axis=0, concat_axis=0, tiled=True),
    )
    work_x, work_do, work_count = (recv_x, recv_do, recv_count)
    count_grid = work_count.astype(jnp.int32)
    slot_ids = jnp.arange(capacity, dtype=jnp.int32)
    is_valid = slot_ids[None, None, :] < count_grid[:, :, None]
    per_expert = jnp.sum(count_grid, axis=0)
    padded = (per_expert + BLOCK - 1) // BLOCK * BLOCK
    begins = jnp.cumsum(padded) - padded
    earlier = jnp.cumsum(count_grid, axis=0) - count_grid
    block_count = buffer_rows // BLOCK + local_experts
    slot_total = block_count * BLOCK
    position = jnp.where(
        is_valid, begins[None, :, None] + earlier[:, :, None] + slot_ids[None, None, :], slot_total
    ).reshape(buffer_rows)
    source_of = (
        jnp.full((slot_total,), buffer_rows, jnp.int32)
        .at[position]
        .set(jnp.arange(buffer_rows, dtype=jnp.int32), mode="drop")
    )
    used_blocks = jnp.sum(padded) // BLOCK
    block_starts = jnp.arange(block_count, dtype=jnp.int32) * BLOCK
    block_expert = jnp.clip(
        jnp.sum((begins[None, :] <= block_starts[:, None]).astype(jnp.int32), axis=1) - 1,
        0,
        local_experts - 1,
    )
    comp_x = take_rows(work_x.reshape(buffer_rows, model_width), source_of, buffer_rows)
    comp_do = take_rows(work_do.reshape(buffer_rows, model_width), source_of, buffer_rows)
    zero_rows = jnp.zeros((slot_total, model_width), jnp.bfloat16)
    zero_hidden = jnp.zeros((slot_total, hidden_units), jnp.bfloat16)

    def block_step(block_id, loop_state):
        out_rows, grad_out, comp_hidden = loop_state
        offset = block_id * BLOCK
        rows_in = lax.dynamic_slice_in_dim(comp_x, offset, BLOCK, 0)
        grads_in = lax.dynamic_slice_in_dim(comp_do, offset, BLOCK, 0)
        expert_id = lax.dynamic_index_in_dim(block_expert, block_id, 0, keepdims=False)
        gate_mat = lax.dynamic_index_in_dim(w_gate, expert_id, 0, keepdims=False)
        up_mat = lax.dynamic_index_in_dim(w_up, expert_id, 0, keepdims=False)
        down_mat = lax.dynamic_index_in_dim(w_down, expert_id, 0, keepdims=False)
        expert_out, grad_rows, hidden_act = expert_block(
            rows_in, grads_in, gate_mat, up_mat, down_mat
        )
        out_rows = lax.dynamic_update_slice_in_dim(out_rows, expert_out, offset, 0)
        grad_out = lax.dynamic_update_slice_in_dim(grad_out, grad_rows, offset, 0)
        comp_hidden = lax.dynamic_update_slice_in_dim(comp_hidden, hidden_act, offset, 0)
        return (out_rows, grad_out, comp_hidden)

    out_rows, grad_out, comp_hidden = lax.fori_loop(
        0, used_blocks, block_step, (zero_rows, zero_rows, zero_hidden)
    )
    slot_owner = jnp.repeat(block_expert, BLOCK)
    partial_down = expert_sums(comp_do, comp_hidden, slot_owner[:, None])
    grad_down = lax.psum_scatter(
        partial_down.astype(jnp.bfloat16), "edata", scatter_dimension=0, tiled=True
    ).astype(jnp.float32)
    ret_o = take_rows(out_rows, position, slot_total).reshape(all_experts, capacity, model_width)
    ret_dx = take_rows(grad_out, position, slot_total).reshape(all_experts, capacity, model_width)
    home_o, home_dx = (
        lax.all_to_all(ret_o, "expert", split_axis=0, concat_axis=0, tiled=True),
        lax.all_to_all(ret_dx, "expert", split_axis=0, concat_axis=0, tiled=True),
    )
    rows_out = jnp.take(home_o.reshape(buffer_rows, model_width), target, axis=0).reshape(
        tok_rows, top_count, model_width
    )
    rows_grad = jnp.take(home_dx.reshape(buffer_rows, model_width), target, axis=0).reshape(
        tok_rows, top_count, model_width
    )
    mixed = jnp.sum(gate_values[:, :, None] * rows_out.astype(jnp.float32), axis=1).astype(
        jnp.bfloat16
    )
    input_grad = jnp.sum(rows_grad.astype(jnp.float32), axis=1).astype(jnp.bfloat16)
    return (mixed, input_grad, grad_down)


def solution(mesh):
    placed = (
        P(("expert", "edata"), None),
        P(("expert", "edata"), None),
        P(("expert", "edata"), None),
        P(("expert", "edata"), None),
        P("expert", None, None),
        P("expert", None, None),
        P("expert", None, None),
    )
    return jax.shard_map(
        shards,
        mesh=mesh,
        in_specs=placed,
        out_specs=(
            P(("expert", "edata"), None),
            P(("expert", "edata"), None),
            P("edata", "expert", None),
        ),
        check_vma=False,
    )
```

profile of v0, /device:TPU:6, one launch (start us, length us, event | category | flops | bytes accessed | tf_op | source)
XLA Modules:
  0.0 341.9 jit_solution(1004589753981535006)
XLA Ops:
  9.9 11.5 %all-to-all-start = ((bf16[32,1,1]{2,1,0:T(2,128)(2,1)}), bf16[32,1,1]{2,1,0:T(2,128)(2,1)S(1)}, u32[]{:S(2)}, u32[]{:S(2)}) async-start(bf16[32,1,1]{2,1,0:T(2,128)(2,1)} %copy.17), calls=%async_computation | async-start | bytes 32768 | tf_op jit(solution)/shard_map/all_to_all | solution.py:85
  26.6 2.5 gather_fusion.1
  31.0 9.4 %all-to-all-start.2 = ((bf16[32,16,2048]{2,1,0:T(8,128)(2,1)}), bf16[32,16,2048]{2,1,0:T(8,128)(2,1)S(1)}, u32[]{:S(2)}, u32[]{:S(2)}) async-start(bf16[32,16,2048]{2,1,0:T(8,128)(2,1)} %select_select_fusion.4), calls=%async_computation.2 | async-start | bytes 4194304 | tf_op jit(solution)/shard_map/all_to_all | solution.py:84
  40.7 3.3 gather_fusion
  44.0 3.3 select_select_fusion.5
  47.3 42.8 %all-to-all-done.2 = bf16[32,16,2048]{2,1,0:T(8,128)(2,1)S(1)} async-done(((bf16[32,16,2048]{2,1,0:T(8,128)(2,1)}), bf16[32,16,2048]{2,1,0:T(8,128)(2,1)S(1)}, u32[]{:S(2)}, u32[]{:S(2)}) %all-to-all-start.2) | async-done | bytes 2097184 | tf_op jit(solution)/shard_map/all_to_all | solution.py:84
  90.1 6.1 %all-to-all-start.1 = ((bf16[32,16,2048]{2,1,0:T(8,128)(2,1)}), bf16[32,16,2048]{2,1,0:T(8,128)(2,1)}, u32[]{:S(2)}, u32[]{:S(2)}) async-start(bf16[32,16,2048]{2,1,0:T(8,128)(2,1)} %select_select_fusion.5), calls=%async_computation.1 | async-start | bytes 4194304 | tf_op jit(solution)/shard_map/all_to_all | solution.py:83
  99.1 2.6 scatter_custom_fusion
  101.9 4.1 %gather_fusion.3 = bf16[640,2048]{1,0:T(8,128)(2,1)} fusion(bf16[512,2048]{1,0:T(8,128)(2,1)S(1)} %bitcast.96, s32[1024]{0:T(1024)S(1)} %pad_clamp_fusion.3), kind=kCustom, calls=%fused_computation.3.clone | custom fusion | bytes 5245440 | tf_op jit(solution)/shard_map/jit(_take)/gather | solution.py:13
  106.0 38.8 %all-to-all-done.1 = bf16[32,16,2048]{2,1,0:T(8,128)(2,1)} async-done(((bf16[32,16,2048]{2,1,0:T(8,128)(2,1)}), bf16[32,16,2048]{2,1,0:T(8,128)(2,1)}, u32[]{:S(2)}, u32[]{:S(2)}) %all-to-all-start.1) | async-done | bytes 2097184 | tf_op jit(solution)/shard_map/all_to_all | solution.py:83
  144.8 8.9 %gather_fusion.2 = bf16[640,2048]{1,0:T(8,128)(2,1)} fusion(bf16[512,2048]{1,0:T(8,128)(2,1)} %bitcast.11, s32[1024]{0:T(1024)S(1)} %pad_clamp_fusion.3), kind=kCustom, calls=%fused_computation.clone | custom fusion | bytes 5245440 | tf_op jit(solution)/shard_map/jit(_take)/gather | solution.py:13
  153.7 4.2 %select_select_fusion = (bf16[640,2048]{1,0:T(8,128)(2,1)}, bf16[640,2048]{1,0:T(8,128)(2,1)}) fusion(bf16[640,2048]{1,0:T(8,128)(2,1)S(1)} %copy-done.5, pred[640]{0:T(1024)(128)(4,1)S(1)} %get-tuple-element.127, pred[640]{0:T(1024)(128)(4,1)S(1)} %get-tuple-element.126, bf16[640,2048]{1,0:T(8,128)(2,1)} %gather_fusion.2), kind=kLoop, calls=%fused_computation.44 | loop fusion | flops 5242880 | bytes 10487040 | tf_op jit(solution)/shard_map/jit(_where)/select_n | solution.py:12
  158.9 1.9 broadcast_in_dim.142.clone
  160.8 1.9 broadcast_in_dim.142
  162.7 22.6 %while.15 = (s32[]{:T(128)}, bf16[640,2048]{1,0:T(8,128)(2,1)}, bf16[640,2048]{1,0:T(8,128)(2,1)}, bf16[640,768]{1,0:T(8,128)(2,1)}, s32[]{:T(128)}, /*index=5*/...) while((s32[]{:T(128)}, bf16[640,2048]{1,0:T(8,128)(2,1)}, ...), condition=%wide.region_10.12_spmd, body=%wide.region_9.11_spmd.sunk | while | flops 2418868224 | bytes 52888828 | solution.py:134
  164.8 2.4 fusion.86
  168.3 2.3 constant_dynamic-update-slice_fusion.2
  170.6 2.0 fusion.88
  176.1 2.4 fusion.86
  179.6 2.3 constant_dynamic-update-slice_fusion.2
  182.0 2.0 fusion.88
  185.3 7.5 %gather_fusion.4 = bf16[512,2048]{1,0:T(8,128)(2,1)} fusion(bf16[640,2048]{1,0:T(8,128)(2,1)} %get-tuple-element.86, s32[1024]{0:T(1024)S(1)} %pad_clamp_fusion.1), kind=kCustom, calls=%fused_computation.1.clone | custom fusion | bytes 4196352 | tf_op jit(solution)/shard_map/jit(_take)/gather | solution.py:13
  192.8 3.3 gather_fusion.6
  196.1 3.9 %select_select_fusion.2 = (bf16[512,2048]{1,0:T(8,128)(2,1)}, bf16[512,2048]{1,0:T(8,128)(2,1)}) fusion(bf16[512,2048]{1,0:T(8,128)(2,1)} %gather_fusion.6, pred[512]{0:T(512)(128)(4,1)S(1)} %compare_and_fusion.2, pred[512]{0:T(512)(128)(4,1)S(1)} %lt.133, bf16[512,2048]{1,0:T(8,128)(2,1)} %gather_fusion.4), kind=kLoop, calls=%fused_computation.50 | loop fusion | flops 4194304 | bytes 8389632 | tf_op jit(solution)/shard_map/jit(_where)/select_n | solution.py:12
  200.0 25.8 %all-to-all-start.3 = ((bf16[32,16,2048]{2,1,0:T(8,128)(2,1)}), bf16[32,16,2048]{2,1,0:T(8,128)(2,1)S(1)}, u32[]{:S(2)}, u32[]{:S(2)}) async-start(bf16[32,16,2048]{2,1,0:T(8,128)(2,1)} %bitcast.99), calls=%async_computation.3 | async-start | bytes 4194304 | tf_op jit(solution)/shard_map/all_to_all | solution.py:145
  225.9 6.2 %fusion.38 = bf16[2048,1,768]{2,0,1:T(8,128)(2,1)} fusion(bf16[640,2048]{1,0:T(8,128)(2,1)} %get-tuple-element.251, bf16[640,768]{1,0:T(8,128)(2,1)S(1)} %copy-done.6, bf16[640]{0:T(1024)(128)(2,1)S(1)} %broadcast_bitcast_fusion), kind=kOutput, calls=%fused_computation.43 | convolution fusion | flops 2015330304 | bytes 6751488 | tf_op jit(solution)/shard_map/rd,rf->df/dot_general | solution.py:41
  232.2 39.9 %all-to-all-done.3 = bf16[32,16,2048]{2,1,0:T(8,128)(2,1)S(1)} async-done(((bf16[32,16,2048]{2,1,0:T(8,128)(2,1)}), bf16[32,16,2048]{2,1,0:T(8,128)(2,1)S(1)}, u32[]{:S(2)}, u32[]{:S(2)}) %all-to-all-start.3) | async-done | bytes 2097184 | tf_op jit(solution)/shard_map/all_to_all | solution.py:145
  272.1 5.5 %all-to-all-start.4 = ((bf16[32,16,2048]{2,1,0:T(8,128)(2,1)}), bf16[32,16,2048]{2,1,0:T(8,128)(2,1)}, u32[]{:S(2)}, u32[]{:S(2)}) async-start(bf16[32,16,2048]{2,1,0:T(8,128)(2,1)} %bitcast.98), calls=%async_computation.4 | async-start | bytes 4194304 | tf_op jit(solution)/shard_map/all_to_all | solution.py:146
  279.0 46.0 %all-to-all-done.4 = bf16[32,16,2048]{2,1,0:T(8,128)(2,1)} async-done(((bf16[32,16,2048]{2,1,0:T(8,128)(2,1)}), bf16[32,16,2048]{2,1,0:T(8,128)(2,1)}, u32[]{:S(2)}, u32[]{:S(2)}) %all-to-all-start.4) | async-done | bytes 2097184 | tf_op jit(solution)/shard_map/all_to_all | solution.py:146
  325.0 4.2 %gather_fusion.7 = bf16[256,2048]{1,0:T(8,128)(2,1)S(1)} fusion(bf16[512,2048]{1,0:T(8,128)(2,1)} %bitcast.19, s32[1024]{0:T(1024)S(1)} %pad_clamp_fusion), kind=kCustom, calls=%fused_computation.5.clone | custom fusion | bytes 2098176 | tf_op jit(solution)/shard_map/jit(_take)/gather | solution.py:151
  330.4 2.1 fusion.39
  332.6 2.5 copy.20
  (84 shorter events, 25.3 us)
Async XLA Ops:
  7.2 33.5 %copy-start = (bf16[32,2048]{1,0:T(8,128)(2,1)S(1)}, bf16[32,2048]{1,0:T(8,128)(2,1)}, u32[]{:S(2)}) copy-start(bf16[32,2048]{1,0:T(8,128)(2,1)} %param.15) | copy-start | bytes 393220
  9.9 21.2 %all-to-all-start = ((bf16[32,1,1]{2,1,0:T(2,128)(2,1)}), bf16[32,1,1]{2,1,0:T(2,128)(2,1)S(1)}, u32[]{:S(2)}, u32[]{:S(2)}) async-start(bf16[32,1,1]{2,1,0:T(2,128)(2,1)} %copy.17), calls=%async_computation | async-start | bytes 32768 | tf_op jit(solution)/shard_map/all_to_all | solution.py:85
  31.0 59.0 %all-to-all-start.2 = ((bf16[32,16,2048]{2,1,0:T(8,128)(2,1)}), bf16[32,16,2048]{2,1,0:T(8,128)(2,1)S(1)}, u32[]{:S(2)}, u32[]{:S(2)}) async-start(bf16[32,16,2048]{2,1,0:T(8,128)(2,1)} %select_select_fusion.4), calls=%async_computation.2 | async-start | bytes 4194304 | tf_op jit(solution)/shard_map/all_to_all | solution.py:84
  90.1 54.7 %all-to-all-start.1 = ((bf16[32,16,2048]{2,1,0:T(8,128)(2,1)}), bf16[32,16,2048]{2,1,0:T(8,128)(2,1)}, u32[]{:S(2)}, u32[]{:S(2)}) async-start(bf16[32,16,2048]{2,1,0:T(8,128)(2,1)} %select_select_fusion.5), calls=%async_computation.1 | async-start | bytes 4194304 | tf_op jit(solution)/shard_map/all_to_all | solution.py:83
  144.8 8.9 %copy-start.5 = (bf16[640,2048]{1,0:T(8,128)(2,1)S(1)}, bf16[640,2048]{1,0:T(8,128)(2,1)}, u32[]{:S(2)}) copy-start(bf16[640,2048]{1,0:T(8,128)(2,1)} %gather_fusion.3) | copy-start | bytes 7864324
  158.9 3.8 %copy-start.1 = (bf16[1,2048,768]{2,1,0:T(8,128)(2,1)S(1)}, bf16[1,2048,768]{2,1,0:T(8,128)(2,1)}, u32[]{:S(2)}) copy-start(bf16[1,2048,768]{2,1,0:T(8,128)(2,1)} %param.19) | copy-start | bytes 9437188
  162.7 2.0 copy-start.2
  164.8 2.4 copy-start.4
  174.0 2.0 copy-start.2
  176.1 2.4 copy-start.4
  185.3 7.5 %copy-start.3 = (bf16[640,2048]{1,0:T(8,128)(2,1)S(1)}, bf16[640,2048]{1,0:T(8,128)(2,1)}, u32[]{:S(2)}) copy-start(bf16[640,2048]{1,0:T(8,128)(2,1)} %get-tuple-element.87) | copy-start | bytes 7864324
  200.0 25.9 %copy-start.6 = (bf16[640,768]{1,0:T(8,128)(2,1)S(1)}, bf16[640,768]{1,0:T(8,128)(2,1)}, u32[]{:S(2)}) copy-start(bf16[640,768]{1,0:T(8,128)(2,1)} %get-tuple-element.88) | copy-start | bytes 2949124
  200.0 72.1 %all-to-all-start.3 = ((bf16[32,16,2048]{2,1,0:T(8,128)(2,1)}), bf16[32,16,2048]{2,1,0:T(8,128)(2,1)S(1)}, u32[]{:S(2)}, u32[]{:S(2)}) async-start(bf16[32,16,2048]{2,1,0:T(8,128)(2,1)} %bitcast.99), calls=%async_computation.3 | async-start | bytes 4194304 | tf_op jit(solution)/shard_map/all_to_all | solution.py:145
  225.8 106.8 %reduce-scatter.2.cloned.1.call-start = ((), (), s32[]{:S(2)}) async-start(), calls=%async_computation.6 | async-start | bytes 3538944 | tf_op jit(solution)/shard_map/reduce_scatter | solution.py:139
  272.1 52.9 %all-to-all-start.4 = ((bf16[32,16,2048]{2,1,0:T(8,128)(2,1)}), bf16[32,16,2048]{2,1,0:T(8,128)(2,1)}, u32[]{:S(2)}, u32[]{:S(2)}) async-start(bf16[32,16,2048]{2,1,0:T(8,128)(2,1)} %bitcast.98), calls=%async_computation.4 | async-start | bytes 4194304 | tf_op jit(solution)/shard_map/all_to_all | solution.py:146
Sparse Core Ops, SparseCore 0:
  232.3 37.3 reduce-scatter.1
where the time goes:
time: 348 us; the launch traced here: 342 us
  waiting for transfers between devices  168 us (48%)
  starting transfers between devices  58.3 us (17%)
  local copies, waits for them, and re-layouts  50 us (14%)
  matrix products  28.2 us (8%)
  other arithmetic  22.5 us (6%)
  between operations  15 us (4%)
    all_to_all x1, waiting for transfers between devices, shards(): lax.all_to_all(ret_dx, 'expert', split_axis=0, concat_axis=0, tiled=True)  46 us
    all_to_all x1, waiting for transfers between devices, shards(): lax.all_to_all(send_do, 'expert', split_axis=0, concat_axis=0, tiled=True)  42.8 us
    all_to_all x1, waiting for transfers between devices, shards(): lax.all_to_all(ret_o, 'expert', split_axis=0, concat_axis=0, tiled=True)  39.9 us
    all_to_all x1, waiting for transfers between devices, shards(): lax.all_to_all(send_x, 'expert', split_axis=0, concat_axis=0, tiled=True)  38.8 us
    gather x6, local copies, waits for them, and re-layouts, take_rows(): jnp.take(source, safe_rows, axis=0)  29.6 us
    all_to_all x1, starting transfers between devices, shards(): lax.all_to_all(ret_o, 'expert', split_axis=0, concat_axis=0, tiled=True)  25.8 us
    select_n x4, other arithmetic, take_rows(): jnp.where(is_valid[:, None], jnp.take(source, safe_rows, axis=0), jnp.zer...  13 us
    all_to_all x1, starting transfers between devices, shards(): lax.all_to_all(send_count, 'expert', split_axis=0, concat_axis=0, tiled=T...  11.5 us
  transfers between devices with their start and end apart: 6, of which 5 were waited for; matrix products, arithmetic and copies ran while one was open for 12% of the time, Pallas kernels for 0%

commit v1 on v0

v1 whole, which is shorter than its diff:
```python
import functools

import jax
import jax.numpy as jnp
from jax import lax
from jax.experimental import pallas as pl
from jax.experimental.pallas import tpu as pltpu
from jax.sharding import PartitionSpec as P

MESH = pl.DeviceIdType.MESH
NZ = 8
NY = 4
SLOTS = 8
F32 = jnp.float32
BF16 = jnp.bfloat16


def position():
    me = lax.axis_index("expert")
    return me // NY, lax.rem(me, NY)


def at_z(z, y, step):
    return lax.rem(z + step + NZ, NZ) * NY + y


def at_y(z, y, step):
    return z * NY + lax.rem(y + step + NY, NY)


def greet(z, y):
    barrier = pltpu.get_barrier_semaphore()
    peers = [at_z(z, y, 1), at_z(z, y, -1)] + [at_y(z, y, j) for j in range(1, NY)]
    for peer in peers:
        pl.semaphore_signal(
            barrier, inc=1, device_id={"expert": peer}, device_id_type=MESH
        )
    pl.semaphore_wait(barrier, len(peers))


def remote(src, dst, send_sem, recv_sem, peer):
    return pltpu.make_async_remote_copy(
        src_ref=src,
        dst_ref=dst,
        send_sem=send_sem,
        recv_sem=recv_sem,
        device_id={"expert": peer},
        device_id_type=MESH,
    )


def ranks_of(gates):
    lanes = gates.shape[1]
    earlier = lax.broadcasted_iota(jnp.int32, (lanes, lanes), 0) < lax.broadcasted_iota(
        jnp.int32, (lanes, lanes), 1
    )
    return jnp.dot(
        (gates > 0).astype(BF16), earlier.astype(BF16), preferred_element_type=F32
    )


def pick_rows(gates_ref, ranks_ref, z, y, tok_rows):
    slot = lax.broadcasted_iota(jnp.int32, (SLOTS, gates_ref.shape[1]), 0).astype(F32)
    picks, weights = [], []
    for j, base in [(j, 0.0) for j in range(NY)] + [(0, float(SLOTS))]:
        expert = at_y(z, y, j)
        gate_row = gates_ref[pl.ds(expert, 1), :]
        rank_row = ranks_ref[pl.ds(expert, 1), :]
        weight = jnp.where(rank_row == slot + base, gate_row, 0.0)
        picks.append(jnp.where(weight > 0, 1.0, 0.0))
        weights.append(jnp.sum(weight, axis=1, keepdims=True))
    picked = jnp.concatenate(picks, axis=0)[:, :tok_rows].astype(BF16)
    return picked, jnp.concatenate(weights, axis=0)


def pick_overflow(gates, ranks, tok_rows):
    rows = [
        jnp.sum(jnp.where(ranks == float(SLOTS + s), gates, 0.0), axis=0, keepdims=True)
        for s in range(SLOTS)
    ]
    weight = jnp.concatenate(rows, axis=0)
    picked = jnp.where(weight > 0, 1.0, 0.0)[:, :tok_rows].astype(BF16)
    return picked, jnp.sum(weight, axis=1, keepdims=True)


def dispatch_kernel(
    x_ref, d_ref, routes_ref, codes_ref,
    rx, rd, vx, vd, gt, flag,
    xg, dg, sx, sd, own, ranks,
    ring_send, ring_recv, y_send, y_recv, v_send, v_recv,
):
    z, y = position()
    tok_rows = x_ref.shape[0]
    experts = gt.shape[1]
    routes = routes_ref[...]
    codes = codes_ref[...].astype(F32)
    gates = codes / jnp.sum(codes, axis=0, keepdims=True)
    expert_ids = lax.broadcasted_iota(jnp.int32, (experts, routes.shape[1]), 0)
    table = jnp.zeros(expert_ids.shape, F32)
    for k in range(routes.shape[0]):
        table = table + jnp.where(
            routes[k : k + 1, :] == expert_ids, gates[k : k + 1, :], 0.0
        )
    gt[0] = table
    greet(z, y)

    right, left = at_z(z, y, 1), at_z(z, y, -1)
    three = pl.ds(1, NY - 1)

    def block(item, r):
        if item == 0:
            return x_ref if r == 0 else xg.at[r]
        if item == 1:
            return d_ref if r == 0 else dg.at[r]
        if item == 2:
            return gt.at[r]
        return (vx if item == 3 else vd).at[r, three]

    half = NZ // 2
    rights, lefts = {}, {}
    for item in range(5):
        long_right = item in (0, 2, 3)
        for s in range(half if long_right else half - 1):
            rights[item, s] = remote(
                block(item, s), block(item, s + 1),
                ring_send.at[item, s], ring_recv.at[item, s + 1], right,
            )
        for s in range(half - 1 if long_right else half):
            r = (NZ - s) % NZ
            lefts[item, s] = remote(
                block(item, r), block(item, NZ - 1 - s),
                ring_send.at[item, half + s], ring_recv.at[item, NZ - 1 - s], left,
            )

    def forward(items, s):
        for item in items:
            for way in (rights, lefts):
                if (item, s) in way:
                    way[item, s].start()

    def arrive(items, s):
        for item in items:
            for way in (rights, lefts):
                if (item, s - 1) in way:
                    way[item, s - 1].wait_recv()

    forward((0, 2, 1), 0)

    rank_own = ranks_of(table)
    ranks[0] = rank_own
    picked, weight = pick_overflow(table, rank_own, tok_rows)
    own[0] = jnp.dot(picked, x_ref[...], preferred_element_type=F32).astype(BF16)
    own[1] = (
        jnp.dot(picked, d_ref[...], preferred_element_type=F32) * weight
    ).astype(BF16)
    v_copies = []
    for j in range(1, NY):
        for i, dst in ((0, vx), (1, vd)):
            copy = remote(
                own.at[i], dst.at[0, j], v_send.at[i, j], v_recv.at[i, j], at_y(z, y, j)
            )
            copy.start()
            v_copies.append(copy)
    mine = table * jnp.where(expert_ids == z * NY + y, 1.0, 0.0)
    count = jnp.sum(jnp.where(mine > 0, 1.0, 0.0))
    flag[...] = jnp.full(flag.shape, count, F32)

    y_copies = []

    def select(r):
        if r:
            ranks[r] = ranks_of(gt[r])
        picked, weight = pick_rows(gt.at[r], ranks.at[r], z, y, tok_rows)
        got_x = jnp.dot(picked, block(0, r)[...], preferred_element_type=F32)
        got_d = jnp.dot(picked, block(1, r)[...], preferred_element_type=F32) * weight
        for i, got, near, over, out in ((0, got_x, rx, vx, sx), (1, got_d, rd, vd, sd)):
            for j in range(1, NY):
                out[r, j] = got[SLOTS * j : SLOTS * (j + 1)].astype(BF16)
                copy = remote(
                    out.at[r, j], near.at[r, j],
                    y_send.at[i, r, j], y_recv.at[i, r, j], at_y(z, y, j),
                )
                copy.start()
                y_copies.append(copy)
            near[r, 0] = got[:SLOTS].astype(BF16)
            over[r, 0] = got[SLOTS * NY :].astype(BF16)

    select(0)
    for copy in v_copies:
        copy.wait_recv()
    forward((3, 4), 0)
    for s in range(1, half):
        arrive((0, 2, 1), s)
        forward((0, 2, 1), s)
        select(s)
        select(NZ - s)
        arrive((3, 4), s)
        forward((3, 4), s)
    arrive((0, 2, 1), half)
    select(half)
    arrive((3, 4), half)
    for copy in y_copies:
        copy.wait_recv()
    for copy in v_copies + y_copies + list(rights.values()) + list(lefts.values()):
        copy.wait_send()


def return_kernel(
    eo, ed, vo, vd, gt,
    mixed, grad,
    bo, bd, part, part_send, over, over_send, last, ranks,
    y_send, y_recv, ring_send, ring_recv, v_send, v_recv,
):
    z, y = position()
    tok_rows = mixed.shape[0]
    half = NZ // 2
    right, left = at_z(z, y, 1), at_z(z, y, -1)
    greet(z, y)
    y_copies = {}
    order = [half]
    for s in range(1, half):
        order += [half + s, half - s]
    order.append(0)
    for r in order:
        for i, src, dst in ((0, eo, bo), (1, ed, bd)):
            for j in range(1, NY):
                copy = remote(
                    src.at[r, j], dst.at[r, j],
                    y_send.at[i, r, j], y_recv.at[i, r, j], at_y(z, y, -j),
                )
                copy.start()
                y_copies[i, r, j] = copy
    for r in range(NZ):
        ranks[r] = ranks_of(gt[r])

    def gathered(i, r):
        picked, weight = pick_rows(gt.at[r], ranks.at[r], z, y, tok_rows)
        back, here, spill = ((bo, eo, vo), (bd, ed, vd))[i]
        for j in range(1, NY):
            y_copies[i, r, j].wait_recv()
        rows = jnp.concatenate(
            [here[r, 0].astype(F32)]
            + [back[r, j].astype(F32) for j in range(1, NY)]
            + [spill[r, 0].astype(F32)],
            axis=0,
        )
        if i == 0:
            rows = rows * weight
        return lax.dot_general(
            picked, rows.astype(BF16), (((0,), (0,)), ((), ())), preferred_element_type=F32
        )

    chains = {
        (0, -1): list(range(half, 0, -1)),
        (0, 1): list(range(half + 1, NZ)),
        (1, -1): list(range(half - 1, 0, -1)),
        (1, 1): list(range(half, NZ)),
    }
    ring, spills = {}, {}
    for (i, way), places in chains.items():
        w = 0 if way < 0 else 1
        peer = left if way < 0 else right
        for r in places:
            to = r + way
            ring[i, way, r] = remote(
                part_send.at[i, w, r], part.at[i, w, to],
                ring_send.at[0, i, w, r], ring_recv.at[0, i, w, to], peer,
            )
            spills[i, way, r] = remote(
                over_send.at[i, w, r], over.at[i, w, to],
                ring_send.at[1, i, w, r], ring_recv.at[1, i, w, to], peer,
            )
    landing = {-1: 0, 1: NZ}
    for s in range(half):
        for (i, way), places in chains.items():
            if s >= len(places):
                continue
            r = places[s]
            w = 0 if way < 0 else 1
            spill = (vo, vd)[i][r, pl.ds(1, NY - 1)]
            if s:
                spills[i, way, places[s - 1]].wait_recv()
                spill = (spill.astype(F32) + over[i, w, r].astype(F32)).astype(BF16)
            over_send[i, w, r] = spill
            spills[i, way, r].start()
            total = gathered(i, r)
            if s:
                ring[i, way, places[s - 1]].wait_recv()
                total = total + part[i, w, r].astype(F32)
            part_send[i, w, r] = total.astype(BF16)
            ring[i, way, r].start()
    totals = [gathered(i, 0) for i in range(2)]
    v_copies = []
    for i in range(2):
        spill = (vo, vd)[i][0, pl.ds(1, NY - 1)].astype(F32)
        for way in (-1, 1):
            spills[i, way, chains[i, way][-1]].wait_recv()
            spill = spill + over[i, 0 if way < 0 else 1, landing[way]].astype(F32)
        over_send[i, 0, 0] = spill.astype(BF16)
        for j in range(1, NY):
            copy = remote(
                over_send.at[i, 0, 0, j - 1], last.at[i, j],
                v_send.at[i, j], v_recv.at[i, j], at_y(z, y, -j),
            )
            copy.start()
            v_copies.append(copy)
    picked, weight = pick_overflow(gt[0], ranks[0], tok_rows)
    for copy in v_copies:
        copy.wait_recv()
    for i, out in ((0, mixed), (1, grad)):
        rows = last[i, 1].astype(F32)
        for j in range(2, NY):
            rows = rows + last[i, j].astype(F32)
        if i == 0:
            rows = rows * weight
        total = totals[i] + lax.dot_general(
            picked, rows.astype(BF16), (((0,), (0,)), ((), ())), preferred_element_type=F32
        )
        for way in (-1, 1):
            ring[i, way, chains[i, way][-1]].wait_recv()
            total = total + part[i, 0 if way < 0 else 1, landing[way]].astype(F32)
        out[...] = total.astype(BF16)
    for copy in (
        list(y_copies.values()) + list(ring.values()) + list(spills.values()) + v_copies
    ):
        copy.wait_send()


def expert_kernel(
    flag, x_ref, d_ref, vx_ref, vd_ref, wg, wu, wd,
    eo, ed, vo, vd, gd,
    acc_o, acc_d, acc_w,
):
    step = pl.program_id(0)
    last = pl.num_programs(0) - 1
    rows = x_ref.shape[0]
    is_hot = flag[0] > float(SLOTS)
    over_cols = (((1,), (1,)), ((), ()))
    over_rows = (((0,), (0,)), ((), ()))

    def part(at, rows_in, grads_in):
        span = pl.ds(at * rows, rows)
        gate_pre = jnp.dot(rows_in[...], wg[...], preferred_element_type=F32)
        up_pre = jnp.dot(rows_in[...], wu[...], preferred_element_type=F32)
        sig = jax.nn.sigmoid(gate_pre)
        act = gate_pre * sig
        hidden = (act * up_pre).astype(BF16)
        out = jnp.dot(hidden, wd[...], preferred_element_type=F32)
        grad_hidden = lax.dot_general(
            grads_in[...], wd[...], over_cols, preferred_element_type=F32
        )
        grad_gate = (grad_hidden * up_pre * sig * (1.0 + gate_pre * (1.0 - sig))).astype(BF16)
        grad_up = (grad_hidden * act).astype(BF16)
        back = lax.dot_general(grad_gate, wg[...], over_cols, preferred_element_type=F32)
        back = back + lax.dot_general(grad_up, wu[...], over_cols, preferred_element_type=F32)

        @pl.when(step == 0)
        def _():
            acc_o[span, :] = out
            acc_d[span, :] = back

        @pl.when(step > 0)
        def _():
            acc_o[span, :] += out
            acc_d[span, :] += back

        return lax.dot_general(grads_in[...], hidden, over_rows, preferred_element_type=F32)

    acc_w[...] = part(0, x_ref, d_ref)

    @pl.when(is_hot)
    def _():
        acc_w[...] += part(1, vx_ref, vd_ref)

    gd[...] = acc_w[...].astype(BF16)

    @pl.when(step == last)
    def _():
        eo[...] = acc_o[:rows, :].astype(BF16)
        ed[...] = acc_d[:rows, :].astype(BF16)

    @pl.when(jnp.logical_and(step == last, is_hot))
    def _():
        vo[...] = acc_o[rows:, :].astype(BF16)
        vd[...] = acc_d[rows:, :].astype(BF16)

    @pl.when(jnp.logical_and(step == last, jnp.logical_not(is_hot)))
    def _():
        vo[...] = jnp.zeros_like(vo)
        vd[...] = jnp.zeros_like(vd)


def shards(tokens, out_grad, routes, gate_codes, w_gate, w_up, w_down):
    tok_rows, width = tokens.shape
    hidden = w_gate.shape[2]
    experts = lax.axis_size("expert")
    lanes = 128
    pad = ((0, 0), (0, lanes - tok_rows))
    routes_t = jnp.pad(routes.T, pad, constant_values=-1)
    codes_t = jnp.pad(gate_codes.T, pad, constant_values=1)
    vmem = pl.BlockSpec(memory_space=pltpu.VMEM)
    row_shape = jax.ShapeDtypeStruct((NZ, NY, SLOTS, width), BF16)
    dma = pltpu.SemaphoreType.DMA
    rx, rd, vx, vd, gt, flag = pl.pallas_call(
        dispatch_kernel,
        out_shape=[row_shape] * 4
        + [
            jax.ShapeDtypeStruct((NZ, experts, lanes), F32),
            jax.ShapeDtypeStruct((8, lanes), F32),
        ],
        in_specs=[vmem] * 4,
        out_specs=[vmem] * 6,
        scratch_shapes=[
            pltpu.VMEM((NZ, tok_rows, width), BF16),
            pltpu.VMEM((NZ, tok_rows, width), BF16),
            pltpu.VMEM((NZ, NY, SLOTS, width), BF16),
            pltpu.VMEM((NZ, NY, SLOTS, width), BF16),
            pltpu.VMEM((2, SLOTS, width), BF16),
            pltpu.VMEM((NZ, experts, lanes), F32),
            dma((5, NZ)),
            dma((5, NZ)),
            dma((2, NZ, NY)),
            dma((2, NZ, NY)),
            dma((2, NY)),
            dma((2, NY)),
        ],
        compiler_params=pltpu.CompilerParams(
            collective_id=0, has_side_effects=True, vmem_limit_bytes=48 << 20
        ),
        name="dispatch",
    )(tokens, out_grad, routes_t, codes_t)

    rows = NZ * NY * SLOTS
    tile = 256
    whole = pl.BlockSpec((rows, width), lambda h, f: (0, 0), pipeline_mode=pl.Buffered(1))
    columns = pl.BlockSpec((None, width, tile), lambda h, f: (0, 0, h))
    eo, ed, vo, ve, gd = pl.pallas_call(
        expert_kernel,
        out_shape=[jax.ShapeDtypeStruct((rows, width), BF16)] * 4
        + [jax.ShapeDtypeStruct((width, hidden), BF16)],
        grid_spec=pltpu.PrefetchScalarGridSpec(
            num_scalar_prefetch=1,
            grid=(hidden // tile,),
            in_specs=[whole] * 4
            + [
                columns,
                columns,
                pl.BlockSpec((None, tile, width), lambda h, f: (0, h, 0)),
            ],
            out_specs=[pl.BlockSpec((rows, width), lambda h, f: (0, 0))] * 4
            + [pl.BlockSpec((width, tile), lambda h, f: (0, h))],
            scratch_shapes=[
                pltpu.VMEM((2 * rows, width), F32),
                pltpu.VMEM((2 * rows, width), F32),
                pltpu.VMEM((width, tile), F32),
            ],
        ),
        compiler_params=pltpu.CompilerParams(
            dimension_semantics=("arbitrary",), vmem_limit_bytes=56 << 20
        ),
        name="experts",
    )(
        flag[0, :1],
        rx.reshape(rows, width),
        rd.reshape(rows, width),
        vx.reshape(rows, width),
        vd.reshape(rows, width),
        w_gate,
        w_up,
        w_down,
    )
    grad_down = lax.psum_scatter(gd, "edata", scatter_dimension=0, tiled=True)

    shape4 = (NZ, NY, SLOTS, width)
    mixed, input_grad = pl.pallas_call(
        return_kernel,
        out_shape=[jax.ShapeDtypeStruct((tok_rows, width), BF16)] * 2,
        in_specs=[vmem] * 5,
        out_specs=[vmem] * 2,
        scratch_shapes=[
            pltpu.VMEM(shape4, BF16),
            pltpu.VMEM(shape4, BF16),
            pltpu.VMEM((2, 2, NZ + 1, tok_rows, width), BF16),
            pltpu.VMEM((2, 2, NZ, tok_rows, width), BF16),
            pltpu.VMEM((2, 2, NZ + 1, NY - 1, SLOTS, width), BF16),
            pltpu.VMEM((2, 2, NZ, NY - 1, SLOTS, width), BF16),
            pltpu.VMEM((2, NY, SLOTS, width), BF16),
            pltpu.VMEM((NZ, experts, lanes), F32),
            dma((2, NZ, NY)),
            dma((2, NZ, NY)),
            dma((2, 2, 2, NZ)),
            dma((2, 2, 2, NZ + 1)),
            dma((2, NY)),
            dma((2, NY)),
        ],
        compiler_params=pltpu.CompilerParams(
            collective_id=1, has_side_effects=True, vmem_limit_bytes=56 << 20
        ),
        name="returns",
    )(
        eo.reshape(shape4), ed.reshape(shape4), vo.reshape(shape4), ve.reshape(shape4), gt
    )
    return (mixed, input_grad, grad_down.astype(F32)[:, None, :])


def solution(mesh):
    placed = (
        P(("expert", "edata"), None),
        P(("expert", "edata"), None),
        P(("expert", "edata"), None),
        P(("expert", "edata"), None),
        P("expert", None, None),
        P("expert", None, None),
        P("expert", None, None),
    )
    return jax.shard_map(
        shards,
        mesh=mesh,
        in_specs=placed,
        out_specs=(
            P(("expert", "edata"), None),
            P(("expert", "edata"), None),
            P("edata", "expert", None),
        ),
        check_vma=False,
    )
```

time: 348 us -> 159 us (0.46)
  waiting for transfers between devices: 168 us -> 0.04 us
  Pallas kernels: 0 us -> 128 us
  starting transfers between devices: 58.3 us -> 0.04 us
  local copies, waits for them, and re-layouts: 50 us -> 13.2 us
  matrix products: 28.2 us -> 0 us
  other arithmetic: 22.5 us -> 1.05 us
    all_to_all x5 -> x0, waiting for transfers between devices: 168 us -> none  [the longest x1 46 us: shards(): lax.all_to_all(ret_dx, 'expert', split_axis=0, concat_axis=0, tiled=True)]
    pallas_call x0 -> x3, Pallas kernels: none -> 128 us  [the longest x1 57.8 us: shards(): pl.pallas_call(return_kernel, out_shape=[jax.ShapeDtypeStruct((tok_rows,...]
    all_to_all x5 -> x0, starting transfers between devices: 58.3 us -> none  [the longest x1 25.8 us: shards(): lax.all_to_all(ret_o, 'expert', split_axis=0, concat_axis=0, tiled=True)]
    gather x8 -> x0, local copies, waits for them, and re-layouts: 35.2 us -> none  [the longest x6 29.6 us: take_rows(): jnp.take(source, safe_rows, axis=0)]
    dot_general x13 -> x0, matrix products: 28.2 us -> none  [the longest x1 6.21 us: expert_sums(): jnp.einsum('rd,rf->df', rows_do, rows_hidden * keep_mask, preferred_eleme...]
    select_n x10 -> x0, other arithmetic: 13 us -> none  [the longest x4 13 us: take_rows(): jnp.where(is_valid[:, None], jnp.take(source, safe_rows, axis=0), jnp.zer...]
    unnamed x12 -> x17, local copies, waits for them, and re-layouts: 3.3 us -> 11.3 us
    broadcast_in_dim x7 -> x0, local copies, waits for them, and re-layouts: 5.15 us -> none  [the longest x2 3.77 us: shards(): zero_rows = jnp.zeros((slot_total, model_width), jnp.bfloat16)]
  transfers between devices with their start and end apart: 6 -> 1, of which waited for: 5 -> 0; matrix products, arithmetic and copies ran while one was open for 12% -> 0% of each run, Pallas kernels for 0% -> 37%
where the time goes in v1:
time: 159 us; the launch traced here: 156 us
  Pallas kernels  128 us (81%)
  between operations  14.1 us (9%)
  local copies, waits for them, and re-layouts  13.2 us (8%)
    pallas_call x1, Pallas kernels, shards(): pl.pallas_call(return_kernel, out_shape=[jax.ShapeDtypeStruct((tok_rows,...  57.8 us
    pallas_call x1, Pallas kernels, shards(): pl.pallas_call(dispatch_kernel, out_shape=[row_shape] * 4 + [jax.ShapeDty...  50.9 us
    pallas_call x1, Pallas kernels, shards(): pl.pallas_call(expert_kernel, out_shape=[jax.ShapeDtypeStruct((rows, widt...  19.1 us
    unnamed x17, local copies, waits for them, and re-layouts  11.3 us
  transfers between devices with their start and end apart: 1, of which 0 were waited for; matrix products, arithmetic and copies ran while one was open for 0% of the time, Pallas kernels for 37%

profile of v1, /device:TPU:6, one launch (start us, length us, event | category | flops | bytes accessed | tf_op | source)
XLA Modules:
  0.0 156.2 jit_solution(13769086658088211646)
XLA Ops:
  7.2 0.0 reduce-scatter.2.cloned.1.call-start
  7.2 0.7 pad.7.routes_ref
  7.9 0.7 pad.8.codes_ref
  8.6 0.0 copy-start.5
  8.6 0.9 copy-done.5
  9.5 0.0 copy-start.6
  9.5 0.9 copy-done.6
  10.4 50.9 %dispatch.1 = (bf16[8,4,8,2048]{3,2,1,0:T(8,128)(2,1)S(1)}, bf16[8,4,8,2048]{3,2,1,0:T(8,128)(2,1)S(1)}, bf16[8,4,8,2048]{3,2,1,0:T(8,128)(2,1)S(1)}, bf16[8,4,8...) custom-call(bf16[32,2048]{1,0:T(8,128)(2,1)S(1)} %copy-done.5, ...), custom_call_target="tpu_custom_call" | custom-call | tf_op jit(solution)/shard_map/dispatch/pallas_call | solution.py:404
  61.4 0.0 copy-start
  61.4 1.0 copy-done
  62.4 0.0 copy-start.1
  62.4 1.1 copy-done.1
  63.4 0.0 copy-start.2
  63.4 1.0 copy-done.2
  64.4 0.0 copy-start.3
  64.4 1.0 copy-done.3
  65.4 0.0 copy-start.4
  65.4 0.7 copy-done.4
  66.0 0.5 slice.3
  66.6 19.1 %experts.1 = (bf16[256,2048]{1,0:T(8,128)(2,1)}, bf16[256,2048]{1,0:T(8,128)(2,1)}, bf16[256,2048]{1,0:T(8,128)(2,1)}, bf16[256,2048]{1,0:T(8,128)(2,1)}, bf16[2048,768]{1,0:T(8,128)(2,1)}) custom-call(f32[1]{0:T(128)} %bitcast.2.flag, bf16[256,2048]{1,0:T(8,128)(2,1)} %bitcast.14, bf16[256,2048]{1,0:T(8,128)(2,1)} %bitcast.15, bf16[256,2048]{1,0:T(8,128)(2,1)} %bitcast.16, ...), custom_call_target="tpu_custom_call" | custom-call | tf_op jit(solution)/shard_map/experts/pallas_call | solution.py:437
  85.6 0.0 reduce-scatter.2.cloned.1.call-update
  85.6 57.8 %returns.1 = (bf16[32,2048]{1,0:T(8,128)(2,1)}, bf16[32,2048]{1,0:T(8,128)(2,1)}) custom-call(bf16[8,4,8,2048]{3,2,1,0:T(8,128)(2,1)} %bitcast.18, bf16[8,4,8,2048]{3,2,1,0:T(8,128)(2,1)} %bitcast.19, bf16[8,4,8,2048]{3,2,1,0:T(8,128)(2,1)} %bitcast.20, bf16[8,4,8,2048]{3,2,1,0:T(8,128)(2,1)} %bitcast.21, f32[8,32,128]{2,1,0:T(8,128)} %copy-done.4), custom_call_target="tpu_custom_call" | custom-call | tf_op jit(solution)/shard_map/returns/pallas_call | solution.py:475
  143.5 0.0 reduce-scatter.2.cloned.1.call-done
  143.5 1.0 bitcast_convert_fusion
  144.6 1.7 %copy.10 = f32[256,1,768]{2,1,0:T(1,128)} copy(f32[256,1,768]{2,0,1:T(8,128)S(1)} %bitcast_convert_fusion) | data formatting | bytes 1572864
  146.2 1.6 %copy.13 = bf16[32,2048]{1,0:T(8,128)(2,1)} copy(bf16[32,2048]{1,0:T(8,128)(2,1)} %get-tuple-element.35) | data formatting | bytes 262144
  147.8 1.6 %copy.14 = bf16[32,2048]{1,0:T(8,128)(2,1)} copy(bf16[32,2048]{1,0:T(8,128)(2,1)} %get-tuple-element.36) | data formatting | bytes 262144
Async XLA Ops:
  7.2 136.3 %reduce-scatter.2.cloned.1.call-start = ((), (), s32[]{:S(2)}) async-start(), calls=%async_computation.1 | async-start | bytes 3538944 | tf_op jit(solution)/shard_map/reduce_scatter | solution.py:472
  8.6 0.9 copy-start.5
  9.5 0.9 copy-start.6
  61.4 1.0 copy-start
  62.4 1.1 copy-start.1
  63.4 1.0 copy-start.2
  64.4 1.0 copy-start.3
  65.4 0.7 copy-start.4
Sparse Core Ops, SparseCore 0:
  85.8 43.3 reduce-scatter.1
